TPU v7x, 256 devices: a whole 4x4x8 slice. The times are simulated.
256 devices in a mesh: row: 16 (over y, z_hi), col: 8 (over x, core), gz: 2 (over z_lo).
Axes of the slice: x: 4, y: 4, z: 8 (z_hi: 4, z_lo: 2; z = z_hi * 2 + z_lo), core: 2. Of those that a mesh axis runs over, the one named last changes fastest.
Arguments:
- source: float32 [2, 4, 1024, 1024], P(None, 'gz', 'row', 'col'), may hold values from -24 to 24
- cell_class: int32 [4, 1024, 1024], P('gz', 'row', 'col'), may hold values from 0 to 7
- coeff_table: float32 [8], replicated, may hold values from 0.5 to 8
- owner_cell: int32 [32768], P(('row', 'col', 'gz')), may hold values from 0 to 16383
- node_pos: float32 [3, 32768], P(None, ('row', 'col', 'gz')), may hold values from 0 to 1
- node_weight: float32 [32768], P(('row', 'col', 'gz')), may hold values from 0.002 to 0.02
Outputs:
- potential: float32 [2, 4, 1024, 1024], P(None, 'gz', 'row', 'col')
- boundary_values: float32 [2, 32768], P(None, ('row', 'col', 'gz'))
Inputs may be any that keep to these rules, and one draw needn't show every extreme that they name: `owner_cell`: each boundary node names a cell of its own device's tile, a flat index over 2 x 64 x 128 cells with the layer slowest.
All inputs are finite; a program needn't handle non-finite values.
Results may differ from a plain program's by a relative error of at most 0.0003.
Values sent between devices are 32-bit elements; how exact they have to be, the bound alone decides.
No kernel may reach another device: no remote copies, remote signals or barrier semaphores. Data moves between devices by JAX's collectives and lax.ppermute only.
A program may use at most 64 MiB of HBM per device.

v0:
```python
import jax
import jax.numpy as jnp
from jax import lax
from jax.sharding import PartitionSpec as P

SWEEPS = 4
OMEGA = 0.8
RELAX = 0.5
SOFTEN = 0.01


def extended(shard, sides, width):
    for axis, dim in sides:
        size, length = (lax.axis_size(axis), shard.shape[dim])
        up = [(i, (i + 1) % size) for i in range(size - 1)]
        down = [(j, i) for i, j in up]
        last = lax.slice_in_dim(shard, length - width, length, axis=dim)
        leading = lax.slice_in_dim(shard, 0, width, axis=dim)
        before = lax.ppermute(last, axis, up)
        after = lax.ppermute(leading, axis, down)
        shard = jnp.concatenate([before, shard, after], axis=dim)
    return shard


def lookup_diagonal(cell_class, coeff_table):
    summed = jnp.zeros(cell_class.shape, jnp.float32)
    for class_level in range(coeff_table.shape[0]):
        summed = summed + jnp.where(
            cell_class == class_level, coeff_table[class_level], jnp.zeros((), coeff_table.dtype)
        )
    return 6.0 + summed


def stencil_update(padded, field, forcing, diagonal):
    beside = padded[:, 2:, 1:-1, 1:-1] + padded[:, :-2, 1:-1, 1:-1]
    beside = beside + padded[:, 1:-1, 2:, 1:-1] + padded[:, 1:-1, :-2, 1:-1]
    beside = beside + padded[:, 1:-1, 1:-1, 2:] + padded[:, 1:-1, 1:-1, :-2]
    return field + OMEGA * (forcing - (diagonal * field - beside)) / diagonal


def sweep_once(field, forcing, diagonal):
    padded = extended(field, (("row", 2), ("col", 3), ("gz", 1)), 1)
    return stencil_update(padded, field, forcing, diagonal)


def on_device(source, cell_class, coeff_table, owner_cell, node_pos, node_weight):
    images, depth, rows_x, cols_y = source.shape
    cell_count = depth * rows_x * cols_y
    node_count = owner_cell.shape[0]
    diagonal = lookup_diagonal(cell_class, coeff_table)

    def relax_all(field, forcing):
        for repeat in range(SWEEPS):
            field = sweep_once(field, forcing, diagonal)
        return field

    target_pos = lax.all_gather(node_pos, ("col", "gz"), axis=1, tiled=True)
    source_meta = lax.all_gather(
        jnp.concatenate([node_pos, node_weight[None, :]], 0), "row", axis=1, tiled=True
    )
    target_count = target_pos.shape[1]
    block_rows = min(512, target_count)
    target_blocks = target_pos.reshape(3, target_count // block_rows, block_rows).transpose(1, 0, 2)

    def kernel_apply(piece_traces):

        def block_sum(target):
            diff_x = target[0][:, None] - source_meta[0][None, :]
            diff_y = target[1][:, None] - source_meta[1][None, :]
            diff_z = target[2][:, None] - source_meta[2][None, :]
            inverse = lax.rsqrt(diff_x * diff_x + diff_y * diff_y + diff_z * diff_z + SOFTEN)
            kernel = source_meta[3][None, :] * diff_z * inverse * inverse * inverse
            return lax.dot_general(
                piece_traces,
                kernel,
                (((1,), (1,)), ((), ())),
                precision=lax.Precision.HIGHEST,
                preferred_element_type=jnp.float32,
            )

        pieces = lax.map(block_sum, target_blocks)
        return pieces.transpose(1, 0, 2).reshape(images, target_count)

    def fk_round(forcing, first, second):
        first = relax_all(first, forcing)
        trace = jnp.take(first.reshape(images, cell_count), owner_cell, axis=1)
        partial_sums = kernel_apply(lax.all_gather(trace, "row", axis=1, tiled=True))
        whole_sums = lax.psum(partial_sums, ("col", "gz"))
        summed = lax.dynamic_slice_in_dim(
            whole_sums, lax.axis_index(("col", "gz")) * node_count, node_count, 1
        )
        values = -0.5 * trace + summed
        spread = (
            jnp.zeros((images, cell_count), jnp.float32)
            .at[:, owner_cell]
            .add(values)
            .reshape(source.shape)
        )
        second = relax_all(second, spread)
        return (first, second, values)

    first = jnp.zeros(source.shape, jnp.float32)
    second = jnp.zeros(source.shape, jnp.float32)
    first, second, values = fk_round(source, first, second)
    forcing = source - RELAX * (first + second)
    first, second, values = fk_round(forcing, first, second)
    return (first + second, values)


def solution(mesh):
    return jax.shard_map(
        on_device,
        mesh=mesh,
        in_specs=(
            P(None, "gz", "row", "col"),
            P("gz", "row", "col"),
            P(),
            P(("row", "col", "gz")),
            P(None, ("row", "col", "gz")),
            P(("row", "col", "gz")),
        ),
        out_specs=(P(None, "gz", "row", "col"), P(None, ("row", "col", "gz"))),
        check_vma=False,
    )
```

profile of v0, /device:TPU:1, one launch (start us, length us, event | category | flops | bytes accessed | tf_op | source)
XLA Modules:
  0.0 793.1 jit_solution(11103989547739344262)
XLA Ops:
  0.7 5.8 collective-permute-start
  7.8 5.8 collective-permute-done.1
  30.7 6.0 broadcast_multiply_fusion
  37.9 5.7 collective-permute-start.6
  93.1 33.6 %all_gather.12 = f32[4,2048]{1,0:T(4,128)S(1)} all-gather(f32[4,128]{1,0:T(4,128)S(1)} %pad_maximum_fusion.298), channel_id=1, replica_groups=mesh['row'=16,'col'=8,'gz'=2] {'row'}, dimensions={1}, use_global_device_ids=true | all-gather | bytes 34816 | tf_op jit(solution)/shard_map/all_gather | solution.py:58
  130.1 29.4 %all_gather.13 = f32[3,2048]{1,0:T(4,128)S(1)} all-gather(f32[3,128]{1,0:T(4,128)S(1)} %copy-done.1), channel_id=1, replica_groups=mesh['row'=16,'col'=8,'gz'=2] {'col','gz'}, dimensions={1}, use_global_device_ids=true | all-gather | bytes 26112 | tf_op jit(solution)/shard_map/all_gather | solution.py:57
  184.9 50.7 %all_gather.14 = f32[2,2048]{0,1:T(8,128)S(1)} all-gather(f32[2,128]{0,1:T(8,128)S(1)} %select_bitcast_fusion.1), channel_id=1, replica_groups=mesh['row'=16,'col'=8,'gz'=2] {'row'}, dimensions={1}, use_global_device_ids=true | all-gather | bytes 17408 | tf_op jit(solution)/shard_map/all_gather | solution.py:87
  236.0 22.4 %while.20 = (s32[]{:T(128)}, f32[4,2,512]{2,1,0:T(2,128)S(1)}, f32[4,2048]{1,0:T(4,128)S(1)}, f32[4,3,512]{2,1,0:T(4,128)S(1)}, f32[2,2048]{1,0:T(2,128)S(1)}, /*index=5*/s32[]{:T(128)}, s32[]{:T(128)}, s32[]{}, s32[]{}) while((s32[]{:T(128)}, f32[4,2,512]{2,1,0:T(2,128)S(1)}, f32[4,2048]{1,0:T(4,128)S(1)}, f32[4,3,512]{2,1,0:T(4,128)S(1)}, ...), condition=%wide.region_1.3_spmd, body=%wide.region_0.2_spmd.sunk | while | flops 38797316 | bytes 137349 | solution.py:81
  236.0 5.5 fusion.246
  241.6 5.5 fusion.246
  247.2 5.5 fusion.246
  252.8 5.5 fusion.246
  258.8 80.7 %psum.14 = f32[2,2048]{0,1:T(8,128)S(1)} all-reduce(f32[2,2048]{0,1:T(8,128)S(1)} %bitcast.103), channel_id=1, replica_groups=mesh['row'=16,'col'=8,'gz'=2] {'col','gz'}, use_global_device_ids=true, to_apply=%region_2.4 | all-reduce | flops 4096 | bytes 32768 | tf_op jit(solution)/shard_map/psum | solution.py:88
  349.6 6.2 collective-permute-start.24
  442.3 5.7 collective-permute-start.48
  453.4 8.3 %collective-permute-start.50 = (f32[2,2,66,1]{3,2,1,0:T(8,128)S(1)}, f32[2,2,66,1]{3,2,1,0:T(8,128)S(1)}, u32[]{:S(2)}, u32[]{:S(2)}) collective-permute-start(f32[2,2,66,1]{3,2,1,0:T(8,128)S(1)} %get-tuple-element.155), channel_id=1, source_target_pairs={{0,2},{2,4},{4,6},{6,8},{8,10},{10,12},{12,14},{1,3},{3,5},{5,7},{... | collective-permute-start | bytes 3176 | tf_op jit(solution)/shard_map/ppermute | solution.py:19
  491.8 5.7 collective-permute-start.66
  513.2 5.7 collective-permute-start.68
  551.2 45.3 %all_gather.15 = f32[2,2048]{0,1:T(8,128)S(1)} all-gather(f32[2,128]{0,1:T(8,128)S(1)} %select_bitcast_fusion), channel_id=1, replica_groups=mesh['row'=16,'col'=8,'gz'=2] {'row'}, dimensions={1}, use_global_device_ids=true | all-gather | bytes 17408 | tf_op jit(solution)/shard_map/all_gather | solution.py:87
  596.9 22.4 %while.21 = (s32[]{:T(128)}, f32[4,2,512]{2,1,0:T(2,128)S(1)}, f32[4,2048]{1,0:T(4,128)S(1)}, f32[4,3,512]{2,1,0:T(4,128)S(1)}, f32[2,2048]{1,0:T(2,128)S(1)}, /*index=5*/s32[]{:T(128)}, s32[]{:T(128)}, s32[]{}, s32[]{}) while((s32[]{:T(128)}, f32[4,2,512]{2,1,0:T(2,128)S(1)}, f32[4,2048]{1,0:T(4,128)S(1)}, f32[4,3,512]{2,1,0:T(4,128)S(1)}, ...), condition=%wide.region_5.7_spmd, body=%wide.region_4.6_spmd.sunk | while | flops 38797316 | bytes 137349 | solution.py:81
  613.7 5.5 fusion.249
  619.6 77.1 %psum.15 = f32[2,2048]{0,1:T(8,128)S(1)} all-reduce(f32[2,2048]{0,1:T(8,128)S(1)} %bitcast.104), channel_id=1, replica_groups=mesh['row'=16,'col'=8,'gz'=2] {'col','gz'}, use_global_device_ids=true, to_apply=%region_6.8 | all-reduce | flops 4096 | bytes 32768 | tf_op jit(solution)/shard_map/psum | solution.py:88
  744.1 5.6 collective-permute-start.80
  772.4 5.6 collective-permute-start.86
  (311 shorter events, 379.9 us)
Async XLA Ops:
  25.4 11.3 %collective-permute-start.4 = (f32[2,1,66,130]{3,2,1,0:T(8,128)S(1)}, f32[2,1,66,130]{3,2,1,0:T(8,128)S(1)}, u32[]{:S(2)}, u32[]{:S(2)}) collective-permute-start(f32[2,1,66,130]{3,2,1,0:T(8,128)S(1)} %get-tuple-element.140), channel_id=1, source_target_pairs={{1,0},{3,2},{5,4},{7,6},{9,8},{11,10},{13,12},{15,14},{17,16},{19,... | collective-permute-start | bytes 205928 | tf_op jit(solution)/shard_map/ppermute | solution.py:20
  26.7 10.0 %collective-permute-start.5 = (f32[2,1,66,130]{3,2,1,0:T(8,128)S(1)}, f32[2,1,66,130]{3,2,1,0:T(8,128)S(1)}, u32[]{:S(2)}, u32[]{:S(2)}) collective-permute-start(f32[2,1,66,130]{3,2,1,0:T(8,128)S(1)} %get-tuple-element.141), channel_id=1, source_target_pairs={{0,1},{2,3},{4,5},{6,7},{8,9},{10,11},{12,13},{14,15},{16,17},{18,... | collective-permute-start | bytes 205928 | tf_op jit(solution)/shard_map/ppermute | solution.py:19
  87.7 39.0 %collective-permute-start.16 = (f32[2,1,66,130]{3,2,1,0:T(8,128)S(1)}, f32[2,1,66,130]{3,2,1,0:T(8,128)S(1)}, u32[]{:S(2)}, u32[]{:S(2)}) collective-permute-start(f32[2,1,66,130]{3,2,1,0:T(8,128)S(1)} %get-tuple-element.136), channel_id=1, source_target_pairs={{1,0},{3,2},{5,4},{7,6},{9,8},{11,10},{13,12},{15,14},{17,16},{19,... | collective-permute-start | bytes 205928 | tf_op jit(solution)/shard_map/ppermute | solution.py:20
  89.0 37.7 %collective-permute-start.17 = (f32[2,1,66,130]{3,2,1,0:T(8,128)S(1)}, f32[2,1,66,130]{3,2,1,0:T(8,128)S(1)}, u32[]{:S(2)}, u32[]{:S(2)}) collective-permute-start(f32[2,1,66,130]{3,2,1,0:T(8,128)S(1)} %get-tuple-element.137), channel_id=1, source_target_pairs={{0,1},{2,3},{4,5},{6,7},{8,9},{10,11},{12,13},{14,15},{16,17},{18,... | collective-permute-start | bytes 205928 | tf_op jit(solution)/shard_map/ppermute | solution.py:19
  127.0 32.5 %collective-permute-start.18 = (f32[2,2,1,128]{3,2,1,0:T(1,128)S(1)}, f32[2,2,1,128]{3,2,1,0:T(1,128)S(1)}, u32[]{:S(2)}, u32[]{:S(2)}) collective-permute-start(f32[2,2,1,128]{3,2,1,0:T(1,128)S(1)} %get-tuple-element.194), channel_id=1, source_target_pairs={{0,16},{16,32},{32,48},{48,64},{64,80},{80,96},{96,112},{112,128},... | collective-permute-start | bytes 6152 | tf_op jit(solution)/shard_map/ppermute | solution.py:19
  128.8 30.7 %collective-permute-start.19 = (f32[2,2,1,128]{3,2,1,0:T(1,128)S(1)}, f32[2,2,1,128]{3,2,1,0:T(1,128)S(1)}, u32[]{:S(2)}, u32[]{:S(2)}) collective-permute-start(f32[2,2,1,128]{3,2,1,0:T(1,128)S(1)} %get-tuple-element.195), channel_id=1, source_target_pairs={{16,0},{32,16},{48,32},{64,48},{80,64},{96,80},{112,96},{128,112},... | collective-permute-start | bytes 6152 | tf_op jit(solution)/shard_map/ppermute | solution.py:20
  378.1 10.9 %collective-permute-start.30 = (f32[2,2,1,128]{3,2,1,0:T(1,128)S(1)}, f32[2,2,1,128]{3,2,1,0:T(1,128)S(1)}, u32[]{:S(2)}, u32[]{:S(2)}) collective-permute-start(f32[2,2,1,128]{3,2,1,0:T(1,128)S(1)} %get-tuple-element.188), channel_id=1, source_target_pairs={{0,16},{16,32},{32,48},{48,64},{64,80},{80,96},{96,112},{112,128},... | collective-permute-start | bytes 6152 | tf_op jit(solution)/shard_map/ppermute | solution.py:19
  382.8 12.7 %collective-permute-start.42 = (f32[2,2,1,128]{3,2,1,0:T(1,128)S(1)}, f32[2,2,1,128]{3,2,1,0:T(1,128)S(1)}, u32[]{:S(2)}, u32[]{:S(2)}) collective-permute-start(f32[2,2,1,128]{3,2,1,0:T(1,128)S(1)} %get-tuple-element.192), channel_id=1, source_target_pairs={{0,16},{16,32},{32,48},{48,64},{64,80},{80,96},{96,112},{112,128},... | collective-permute-start | bytes 6152 | tf_op jit(solution)/shard_map/ppermute | solution.py:19
  400.3 9.9 %collective-permute-start.34 = (f32[2,1,66,130]{3,2,1,0:T(8,128)S(1)}, f32[2,1,66,130]{3,2,1,0:T(8,128)S(1)}, u32[]{:S(2)}, u32[]{:S(2)}) collective-permute-start(f32[2,1,66,130]{3,2,1,0:T(8,128)S(1)} %get-tuple-element.128), channel_id=1, source_target_pairs={{1,0},{3,2},{5,4},{7,6},{9,8},{11,10},{13,12},{15,14},{17,16},{19,... | collective-permute-start | bytes 205928 | tf_op jit(solution)/shard_map/ppermute | solution.py:20
  405.8 11.1 %collective-permute-start.44 = (f32[2,2,66,1]{3,2,1,0:T(8,128)S(1)}, f32[2,2,66,1]{3,2,1,0:T(8,128)S(1)}, u32[]{:S(2)}, u32[]{:S(2)}) collective-permute-start(f32[2,2,66,1]{3,2,1,0:T(8,128)S(1)} %get-tuple-element.163), channel_id=1, source_target_pairs={{0,2},{2,4},{4,6},{6,8},{8,10},{10,12},{12,14},{1,3},{3,5},{5,7},{... | collective-permute-start | bytes 3176 | tf_op jit(solution)/shard_map/ppermute | solution.py:19
  422.1 12.0 %collective-permute-start.38 = (f32[2,2,66,1]{3,2,1,0:T(8,128)S(1)}, f32[2,2,66,1]{3,2,1,0:T(8,128)S(1)}, u32[]{:S(2)}, u32[]{:S(2)}) collective-permute-start(f32[2,2,66,1]{3,2,1,0:T(8,128)S(1)} %get-tuple-element.157), channel_id=1, source_target_pairs={{0,2},{2,4},{4,6},{6,8},{8,10},{10,12},{12,14},{1,3},{3,5},{5,7},{... | collective-permute-start | bytes 3176 | tf_op jit(solution)/shard_map/ppermute | solution.py:19
  428.9 10.9 %collective-permute-start.46 = (f32[2,1,66,130]{3,2,1,0:T(8,128)S(1)}, f32[2,1,66,130]{3,2,1,0:T(8,128)S(1)}, u32[]{:S(2)}, u32[]{:S(2)}) collective-permute-start(f32[2,1,66,130]{3,2,1,0:T(8,128)S(1)} %get-tuple-element.132), channel_id=1, source_target_pairs={{1,0},{3,2},{5,4},{7,6},{9,8},{11,10},{13,12},{15,14},{17,16},{19,... | collective-permute-start | bytes 205928 | tf_op jit(solution)/shard_map/ppermute | solution.py:20
  430.2 9.6 %collective-permute-start.47 = (f32[2,1,66,130]{3,2,1,0:T(8,128)S(1)}, f32[2,1,66,130]{3,2,1,0:T(8,128)S(1)}, u32[]{:S(2)}, u32[]{:S(2)}) collective-permute-start(f32[2,1,66,130]{3,2,1,0:T(8,128)S(1)} %get-tuple-element.133), channel_id=1, source_target_pairs={{0,1},{2,3},{4,5},{6,7},{8,9},{10,11},{12,13},{14,15},{16,17},{18,... | collective-permute-start | bytes 205928 | tf_op jit(solution)/shard_map/ppermute | solution.py:19
  453.4 10.4 %collective-permute-start.50 = (f32[2,2,66,1]{3,2,1,0:T(8,128)S(1)}, f32[2,2,66,1]{3,2,1,0:T(8,128)S(1)}, u32[]{:S(2)}, u32[]{:S(2)}) collective-permute-start(f32[2,2,66,1]{3,2,1,0:T(8,128)S(1)} %get-tuple-element.155), channel_id=1, source_target_pairs={{0,2},{2,4},{4,6},{6,8},{8,10},{10,12},{12,14},{1,3},{3,5},{5,7},{... | collective-permute-start | bytes 3176 | tf_op jit(solution)/shard_map/ppermute | solution.py:19
  485.4 13.4 %collective-permute-start.56 = (f32[2,2,66,1]{3,2,1,0:T(8,128)S(1)}, f32[2,2,66,1]{3,2,1,0:T(8,128)S(1)}, u32[]{:S(2)}, u32[]{:S(2)}) collective-permute-start(f32[2,2,66,1]{3,2,1,0:T(8,128)S(1)} %get-tuple-element.153), channel_id=1, source_target_pairs={{0,2},{2,4},{4,6},{6,8},{8,10},{10,12},{12,14},{1,3},{3,5},{5,7},{... | collective-permute-start | bytes 3176 | tf_op jit(solution)/shard_map/ppermute | solution.py:19
  489.8 9.0 %collective-permute-start.57 = (f32[2,2,66,1]{3,2,1,0:T(8,128)S(1)}, f32[2,2,66,1]{3,2,1,0:T(8,128)S(1)}, u32[]{:S(2)}, u32[]{:S(2)}) collective-permute-start(f32[2,2,66,1]{3,2,1,0:T(8,128)S(1)} %get-tuple-element.152), channel_id=1, source_target_pairs={{2,0},{4,2},{6,4},{8,6},{10,8},{12,10},{14,12},{3,1},{5,3},{7,5},{... | collective-permute-start | bytes 3176 | tf_op jit(solution)/shard_map/ppermute | solution.py:20
  491.8 12.7 %collective-permute-start.66 = (f32[2,2,1,128]{3,2,1,0:T(1,128)S(1)}, f32[2,2,1,128]{3,2,1,0:T(1,128)S(1)}, u32[]{:S(2)}, u32[]{:S(2)}) collective-permute-start(f32[2,2,1,128]{3,2,1,0:T(1,128)S(1)} %get-tuple-element.178), channel_id=1, source_target_pairs={{0,16},{16,32},{32,48},{48,64},{64,80},{80,96},{96,112},{112,128},... | collective-permute-start | bytes 6152 | tf_op jit(solution)/shard_map/ppermute | solution.py:19
  506.9 13.9 %collective-permute-start.60 = (f32[2,2,1,128]{3,2,1,0:T(1,128)S(1)}, f32[2,2,1,128]{3,2,1,0:T(1,128)S(1)}, u32[]{:S(2)}, u32[]{:S(2)}) collective-permute-start(f32[2,2,1,128]{3,2,1,0:T(1,128)S(1)} %get-tuple-element.180), channel_id=1, source_target_pairs={{0,16},{16,32},{32,48},{48,64},{64,80},{80,96},{96,112},{112,128},... | collective-permute-start | bytes 6152 | tf_op jit(solution)/shard_map/ppermute | solution.py:19
  511.8 9.1 %collective-permute-start.61 = (f32[2,2,1,128]{3,2,1,0:T(1,128)S(1)}, f32[2,2,1,128]{3,2,1,0:T(1,128)S(1)}, u32[]{:S(2)}, u32[]{:S(2)}) collective-permute-start(f32[2,2,1,128]{3,2,1,0:T(1,128)S(1)} %get-tuple-element.181), channel_id=1, source_target_pairs={{16,0},{32,16},{48,32},{64,48},{80,64},{96,80},{112,96},{128,112},... | collective-permute-start | bytes 6152 | tf_op jit(solution)/shard_map/ppermute | solution.py:20
  513.2 13.4 %collective-permute-start.68 = (f32[2,2,66,1]{3,2,1,0:T(8,128)S(1)}, f32[2,2,66,1]{3,2,1,0:T(8,128)S(1)}, u32[]{:S(2)}, u32[]{:S(2)}) collective-permute-start(f32[2,2,66,1]{3,2,1,0:T(8,128)S(1)} %get-tuple-element.149), channel_id=1, source_target_pairs={{0,2},{2,4},{4,6},{6,8},{8,10},{10,12},{12,14},{1,3},{3,5},{5,7},{... | collective-permute-start | bytes 3176 | tf_op jit(solution)/shard_map/ppermute | solution.py:19
  531.3 10.8 %collective-permute-start.64 = (f32[2,1,66,130]{3,2,1,0:T(8,128)S(1)}, f32[2,1,66,130]{3,2,1,0:T(8,128)S(1)}, u32[]{:S(2)}, u32[]{:S(2)}) collective-permute-start(f32[2,1,66,130]{3,2,1,0:T(8,128)S(1)} %get-tuple-element.120), channel_id=1, source_target_pairs={{1,0},{3,2},{5,4},{7,6},{9,8},{11,10},{13,12},{15,14},{17,16},{19,... | collective-permute-start | bytes 205928 | tf_op jit(solution)/shard_map/ppermute | solution.py:20
  532.6 9.5 %collective-permute-start.65 = (f32[2,1,66,130]{3,2,1,0:T(8,128)S(1)}, f32[2,1,66,130]{3,2,1,0:T(8,128)S(1)}, u32[]{:S(2)}, u32[]{:S(2)}) collective-permute-start(f32[2,1,66,130]{3,2,1,0:T(8,128)S(1)} %get-tuple-element.121), channel_id=1, source_target_pairs={{0,1},{2,3},{4,5},{6,7},{8,9},{10,11},{12,13},{14,15},{16,17},{18,... | collective-permute-start | bytes 205928 | tf_op jit(solution)/shard_map/ppermute | solution.py:19
  536.8 170.1 %collective-permute-start.70 = (f32[2,1,66,130]{3,2,1,0:T(8,128)S(1)}, f32[2,1,66,130]{3,2,1,0:T(8,128)S(1)}, u32[]{:S(2)}, u32[]{:S(2)}) collective-permute-start(f32[2,1,66,130]{3,2,1,0:T(8,128)S(1)} %get-tuple-element.118), channel_id=1, source_target_pairs={{1,0},{3,2},{5,4},{7,6},{9,8},{11,10},{13,12},{15,14},{17,16},{19,... | collective-permute-start | bytes 205928 | tf_op jit(solution)/shard_map/ppermute | solution.py:20
  538.1 168.8 %collective-permute-start.71 = (f32[2,1,66,130]{3,2,1,0:T(8,128)S(1)}, f32[2,1,66,130]{3,2,1,0:T(8,128)S(1)}, u32[]{:S(2)}, u32[]{:S(2)}) collective-permute-start(f32[2,1,66,130]{3,2,1,0:T(8,128)S(1)} %get-tuple-element.119), channel_id=1, source_target_pairs={{0,1},{2,3},{4,5},{6,7},{8,9},{10,11},{12,13},{14,15},{16,17},{18,... | collective-permute-start | bytes 205928 | tf_op jit(solution)/shard_map/ppermute | solution.py:19
  (70 other events, 719.7 us)
where the time goes:
time: 796 us; the launch traced here: 793 us
  blocking collectives  317 us (40%)
  starting transfers between devices  269 us (34%)
  waiting for transfers between devices  102 us (13%)
  matrix products  44.2 us (6%)
  local copies, waits for them, and re-layouts  33.9 us (4%)
  other arithmetic  24.6 us (3%)
    ppermute x45, starting transfers between devices, extended(): before = lax.ppermute(last, axis, up)  194 us
    psum x2, blocking collectives, fk_round(): whole_sums = lax.psum(partial_sums, ('col', 'gz'))  158 us
    all_gather x2, blocking collectives, fk_round(): lax.all_gather(trace, 'row', axis=1, tiled=True)  96 us
    ppermute x45, waiting for transfers between devices, extended(): after = lax.ppermute(leading, axis, down)  88.5 us
    ppermute x45, starting transfers between devices, extended(): after = lax.ppermute(leading, axis, down)  75.6 us
    dot_general x8, matrix products, block_sum(): lax.dot_general(piece_traces, kernel, (((1,), (1,)), ((), ())), precision...  44.2 us
    all_gather x1, blocking collectives, on_device(): lax.all_gather(jnp.concatenate([node_pos, node_weight[None, :]], 0), 'row...  33.6 us
    all_gather x1, blocking collectives, on_device(): target_pos = lax.all_gather(node_pos, ('col', 'gz'), axis=1, tiled=True)  29.4 us
  transfers between devices with their start and end apart: 90, of which 44 were waited for; matrix products, arithmetic and copies ran while one was open for 7% of the time, Pallas kernels for 0%

commit v1 on v0

--- a/solution.py
+++ b/solution.py
@@ -85,7 +85,7 @@
         first = relax_all(first, forcing)
         trace = jnp.take(first.reshape(images, cell_count), owner_cell, axis=1)
         partial_sums = kernel_apply(lax.all_gather(trace, "row", axis=1, tiled=True))
-        whole_sums = lax.psum(partial_sums, ("col", "gz"))
+        whole_sums = jnp.sum(lax.all_gather(partial_sums, ("col", "gz")), axis=0)
         summed = lax.dynamic_slice_in_dim(
             whole_sums, lax.axis_index(("col", "gz")) * node_count, node_count, 1
         )

time: 796 us -> 697 us (0.88)
  blocking collectives: 317 us -> 225 us
  starting transfers between devices: 269 us -> 259 us
    psum x2 -> x0, blocking collectives: 158 us -> none  [fk_round(): whole_sums = lax.psum(partial_sums, ('col', 'gz'))]
    all_gather x0 -> x2, blocking collectives: none -> 61.8 us  [fk_round(): whole_sums = jnp.sum(lax.all_gather(partial_sums, ('col', 'gz')), axis=0)]
  transfers between devices with their start and end apart: 90 -> 90, of which waited for: 44 -> 43; matrix products, arithmetic and copies ran while one was open for 7% -> 7% of each run, Pallas kernels for 0% -> 0%
where the time goes in v1:
time: 697 us; the launch traced here: 694 us
  starting transfers between devices  259 us (37%)
  blocking collectives  225 us (32%)
  waiting for transfers between devices  105 us (15%)
  matrix products  44.2 us (6%)
  local copies, waits for them, and re-layouts  33.3 us (5%)
  other arithmetic  24.7 us (4%)
    ppermute x45, starting transfers between devices, extended(): before = lax.ppermute(last, axis, up)  186 us
    all_gather x2, blocking collectives, fk_round(): lax.all_gather(trace, 'row', axis=1, tiled=True)  99.9 us
    ppermute x45, waiting for transfers between devices, extended(): after = lax.ppermute(leading, axis, down)  91 us
    ppermute x45, starting transfers between devices, extended(): after = lax.ppermute(leading, axis, down)  73.5 us
    all_gather x2, blocking collectives, fk_round(): whole_sums = jnp.sum(lax.all_gather(partial_sums, ('col', 'gz')), axis=0)  61.8 us
    dot_general x8, matrix products, block_sum(): lax.dot_general(piece_traces, kernel, (((1,), (1,)), ((), ())), precision...  44.2 us
    all_gather x1, blocking collectives, on_device(): lax.all_gather(jnp.concatenate([node_pos, node_weight[None, :]], 0), 'row...  33.6 us
    all_gather x1, blocking collectives, on_device(): target_pos = lax.all_gather(node_pos, ('col', 'gz'), axis=1, tiled=True)  29.4 us
  transfers between devices with their start and end apart: 90, of which 43 were waited for; matrix products, arithmetic and copies ran while one was open for 7% of the time, Pallas kernels for 0%

profile of v1, /device:TPU:1, one launch (start us, length us, event | category | flops | bytes accessed | tf_op | source)
XLA Modules:
  0.0 694.1 jit_solution(7293898002494712638)
XLA Ops:
  0.7 5.8 collective-permute-start
  7.8 5.8 collective-permute-done.1
  30.7 6.0 broadcast_multiply_fusion
  37.9 5.7 collective-permute-start.6
  93.1 33.6 %all_gather.18 = f32[4,2048]{1,0:T(4,128)S(1)} all-gather(f32[4,128]{1,0:T(4,128)S(1)} %pad_maximum_fusion.298), channel_id=1, replica_groups=mesh['row'=16,'col'=8,'gz'=2] {'row'}, dimensions={1}, use_global_device_ids=true | all-gather | bytes 34816 | tf_op jit(solution)/shard_map/all_gather | solution.py:58
  130.1 29.4 %all_gather.19 = f32[3,2048]{1,0:T(4,128)S(1)} all-gather(f32[3,128]{1,0:T(4,128)S(1)} %copy-done.1), channel_id=1, replica_groups=mesh['row'=16,'col'=8,'gz'=2] {'col','gz'}, dimensions={1}, use_global_device_ids=true | all-gather | bytes 26112 | tf_op jit(solution)/shard_map/all_gather | solution.py:57
  184.9 50.7 %all_gather.20 = f32[2,2048]{0,1:T(8,128)S(1)} all-gather(f32[2,128]{0,1:T(8,128)S(1)} %select_bitcast_fusion.1), channel_id=1, replica_groups=mesh['row'=16,'col'=8,'gz'=2] {'row'}, dimensions={1}, use_global_device_ids=true | all-gather | bytes 17408 | tf_op jit(solution)/shard_map/all_gather | solution.py:87
  236.0 22.4 %while.20 = (s32[]{:T(128)}, f32[4,2,512]{2,1,0:T(2,128)S(1)}, f32[4,2048]{1,0:T(4,128)S(1)}, f32[4,3,512]{2,1,0:T(4,128)S(1)}, f32[2,2048]{1,0:T(2,128)S(1)}, /*index=5*/s32[]{:T(128)}, s32[]{:T(128)}, s32[]{}, s32[]{}) while((s32[]{:T(128)}, f32[4,2,512]{2,1,0:T(2,128)S(1)}, f32[4,2048]{1,0:T(4,128)S(1)}, f32[4,3,512]{2,1,0:T(4,128)S(1)}, ...), condition=%wide.region_1.3_spmd, body=%wide.region_0.2_spmd.sunk | while | flops 38797316 | bytes 137349 | solution.py:81
  236.0 5.5 fusion.245
  241.6 5.5 fusion.245
  247.2 5.5 fusion.245
  252.8 5.5 fusion.245
  258.4 33.2 %all_gather.21 = f32[16,2,2048]{2,1,0:T(2,128)S(1)} all-gather(f32[1,2,2048]{2,1,0:T(2,128)S(1)} %bitcast.114), channel_id=1, replica_groups=mesh['row'=16,'col'=8,'gz'=2] {'col','gz'}, dimensions={0}, use_global_device_ids=true | all-gather | bytes 278528 | tf_op jit(solution)/shard_map/all_gather | solution.py:88
  361.3 5.8 collective-permute-start.36
  394.1 5.5 collective-permute-start.48
  405.0 6.8 collective-permute-start.50
  442.5 5.7 collective-permute-start.66
  501.7 49.2 %all_gather.22 = f32[2,2048]{0,1:T(8,128)S(1)} all-gather(f32[2,128]{0,1:T(8,128)S(1)} %select_bitcast_fusion), channel_id=1, replica_groups=mesh['row'=16,'col'=8,'gz'=2] {'row'}, dimensions={1}, use_global_device_ids=true | all-gather | bytes 17408 | tf_op jit(solution)/shard_map/all_gather | solution.py:87
  551.2 22.4 %while.21 = (s32[]{:T(128)}, f32[4,2,512]{2,1,0:T(2,128)S(1)}, f32[4,2048]{1,0:T(4,128)S(1)}, f32[4,3,512]{2,1,0:T(4,128)S(1)}, f32[2,2048]{1,0:T(2,128)S(1)}, /*index=5*/s32[]{:T(128)}, s32[]{:T(128)}, s32[]{}, s32[]{}) while((s32[]{:T(128)}, f32[4,2,512]{2,1,0:T(2,128)S(1)}, f32[4,2048]{1,0:T(4,128)S(1)}, f32[4,3,512]{2,1,0:T(4,128)S(1)}, ...), condition=%wide.region_5.7_spmd, body=%wide.region_4.6_spmd.sunk | while | flops 38797316 | bytes 137349 | solution.py:81
  551.3 5.5 fusion.248
  556.9 5.5 fusion.248
  562.5 5.5 fusion.248
  568.1 5.5 fusion.248
  573.6 28.6 %all_gather.23 = f32[16,2,2048]{2,1,0:T(2,128)S(1)} all-gather(f32[1,2,2048]{2,1,0:T(2,128)S(1)} %bitcast.115), channel_id=1, replica_groups=mesh['row'=16,'col'=8,'gz'=2] {'col','gz'}, dimensions={0}, use_global_device_ids=true | all-gather | bytes 278528 | tf_op jit(solution)/shard_map/all_gather | solution.py:88
  (315 shorter events, 375.5 us)
Async XLA Ops:
  25.4 11.3 %collective-permute-start.4 = (f32[2,1,66,130]{3,2,1,0:T(8,128)S(1)}, f32[2,1,66,130]{3,2,1,0:T(8,128)S(1)}, u32[]{:S(2)}, u32[]{:S(2)}) collective-permute-start(f32[2,1,66,130]{3,2,1,0:T(8,128)S(1)} %get-tuple-element.164), channel_id=1, source_target_pairs={{1,0},{3,2},{5,4},{7,6},{9,8},{11,10},{13,12},{15,14},{17,16},{19,... | collective-permute-start | bytes 205928 | tf_op jit(solution)/shard_map/ppermute | solution.py:20
  26.7 10.0 %collective-permute-start.5 = (f32[2,1,66,130]{3,2,1,0:T(8,128)S(1)}, f32[2,1,66,130]{3,2,1,0:T(8,128)S(1)}, u32[]{:S(2)}, u32[]{:S(2)}) collective-permute-start(f32[2,1,66,130]{3,2,1,0:T(8,128)S(1)} %get-tuple-element.165), channel_id=1, source_target_pairs={{0,1},{2,3},{4,5},{6,7},{8,9},{10,11},{12,13},{14,15},{16,17},{18,... | collective-permute-start | bytes 205928 | tf_op jit(solution)/shard_map/ppermute | solution.py:19
  87.7 39.0 %collective-permute-start.16 = (f32[2,1,66,130]{3,2,1,0:T(8,128)S(1)}, f32[2,1,66,130]{3,2,1,0:T(8,128)S(1)}, u32[]{:S(2)}, u32[]{:S(2)}) collective-permute-start(f32[2,1,66,130]{3,2,1,0:T(8,128)S(1)} %get-tuple-element.160), channel_id=1, source_target_pairs={{1,0},{3,2},{5,4},{7,6},{9,8},{11,10},{13,12},{15,14},{17,16},{19,... | collective-permute-start | bytes 205928 | tf_op jit(solution)/shard_map/ppermute | solution.py:20
  89.0 37.7 %collective-permute-start.17 = (f32[2,1,66,130]{3,2,1,0:T(8,128)S(1)}, f32[2,1,66,130]{3,2,1,0:T(8,128)S(1)}, u32[]{:S(2)}, u32[]{:S(2)}) collective-permute-start(f32[2,1,66,130]{3,2,1,0:T(8,128)S(1)} %get-tuple-element.161), channel_id=1, source_target_pairs={{0,1},{2,3},{4,5},{6,7},{8,9},{10,11},{12,13},{14,15},{16,17},{18,... | collective-permute-start | bytes 205928 | tf_op jit(solution)/shard_map/ppermute | solution.py:19
  127.0 32.5 %collective-permute-start.18 = (f32[2,2,1,128]{3,2,1,0:T(1,128)S(1)}, f32[2,2,1,128]{3,2,1,0:T(1,128)S(1)}, u32[]{:S(2)}, u32[]{:S(2)}) collective-permute-start(f32[2,2,1,128]{3,2,1,0:T(1,128)S(1)} %get-tuple-element.218), channel_id=1, source_target_pairs={{0,16},{16,32},{32,48},{48,64},{64,80},{80,96},{96,112},{112,128},... | collective-permute-start | bytes 6152 | tf_op jit(solution)/shard_map/ppermute | solution.py:19
  128.8 30.7 %collective-permute-start.19 = (f32[2,2,1,128]{3,2,1,0:T(1,128)S(1)}, f32[2,2,1,128]{3,2,1,0:T(1,128)S(1)}, u32[]{:S(2)}, u32[]{:S(2)}) collective-permute-start(f32[2,2,1,128]{3,2,1,0:T(1,128)S(1)} %get-tuple-element.219), channel_id=1, source_target_pairs={{16,0},{32,16},{48,32},{64,48},{80,64},{96,80},{112,96},{128,112},... | collective-permute-start | bytes 6152 | tf_op jit(solution)/shard_map/ppermute | solution.py:20
  330.5 10.4 %collective-permute-start.30 = (f32[2,2,1,128]{3,2,1,0:T(1,128)S(1)}, f32[2,2,1,128]{3,2,1,0:T(1,128)S(1)}, u32[]{:S(2)}, u32[]{:S(2)}) collective-permute-start(f32[2,2,1,128]{3,2,1,0:T(1,128)S(1)} %get-tuple-element.212), channel_id=1, source_target_pairs={{0,16},{16,32},{32,48},{48,64},{64,80},{80,96},{96,112},{112,128},... | collective-permute-start | bytes 6152 | tf_op jit(solution)/shard_map/ppermute | solution.py:19
  334.7 11.7 %collective-permute-start.42 = (f32[2,2,1,128]{3,2,1,0:T(1,128)S(1)}, f32[2,2,1,128]{3,2,1,0:T(1,128)S(1)}, u32[]{:S(2)}, u32[]{:S(2)}) collective-permute-start(f32[2,2,1,128]{3,2,1,0:T(1,128)S(1)} %get-tuple-element.216), channel_id=1, source_target_pairs={{0,16},{16,32},{32,48},{48,64},{64,80},{80,96},{96,112},{112,128},... | collective-permute-start | bytes 6152 | tf_op jit(solution)/shard_map/ppermute | solution.py:19
  351.1 9.9 %collective-permute-start.34 = (f32[2,1,66,130]{3,2,1,0:T(8,128)S(1)}, f32[2,1,66,130]{3,2,1,0:T(8,128)S(1)}, u32[]{:S(2)}, u32[]{:S(2)}) collective-permute-start(f32[2,1,66,130]{3,2,1,0:T(8,128)S(1)} %get-tuple-element.152), channel_id=1, source_target_pairs={{1,0},{3,2},{5,4},{7,6},{9,8},{11,10},{13,12},{15,14},{17,16},{19,... | collective-permute-start | bytes 205928 | tf_op jit(solution)/shard_map/ppermute | solution.py:20
  356.6 11.7 %collective-permute-start.44 = (f32[2,2,66,1]{3,2,1,0:T(8,128)S(1)}, f32[2,2,66,1]{3,2,1,0:T(8,128)S(1)}, u32[]{:S(2)}, u32[]{:S(2)}) collective-permute-start(f32[2,2,66,1]{3,2,1,0:T(8,128)S(1)} %get-tuple-element.187), channel_id=1, source_target_pairs={{0,2},{2,4},{4,6},{6,8},{8,10},{10,12},{12,14},{1,3},{3,5},{5,7},{... | collective-permute-start | bytes 3176 | tf_op jit(solution)/shard_map/ppermute | solution.py:19
  358.9 9.5 %collective-permute-start.45 = (f32[2,2,66,1]{3,2,1,0:T(8,128)S(1)}, f32[2,2,66,1]{3,2,1,0:T(8,128)S(1)}, u32[]{:S(2)}, u32[]{:S(2)}) collective-permute-start(f32[2,2,66,1]{3,2,1,0:T(8,128)S(1)} %get-tuple-element.186), channel_id=1, source_target_pairs={{2,0},{4,2},{6,4},{8,6},{10,8},{12,10},{14,12},{3,1},{5,3},{7,5},{... | collective-permute-start | bytes 3176 | tf_op jit(solution)/shard_map/ppermute | solution.py:20
  374.1 11.7 %collective-permute-start.38 = (f32[2,2,66,1]{3,2,1,0:T(8,128)S(1)}, f32[2,2,66,1]{3,2,1,0:T(8,128)S(1)}, u32[]{:S(2)}, u32[]{:S(2)}) collective-permute-start(f32[2,2,66,1]{3,2,1,0:T(8,128)S(1)} %get-tuple-element.181), channel_id=1, source_target_pairs={{0,2},{2,4},{4,6},{6,8},{8,10},{10,12},{12,14},{1,3},{3,5},{5,7},{... | collective-permute-start | bytes 3176 | tf_op jit(solution)/shard_map/ppermute | solution.py:19
  380.5 10.9 %collective-permute-start.46 = (f32[2,1,66,130]{3,2,1,0:T(8,128)S(1)}, f32[2,1,66,130]{3,2,1,0:T(8,128)S(1)}, u32[]{:S(2)}, u32[]{:S(2)}) collective-permute-start(f32[2,1,66,130]{3,2,1,0:T(8,128)S(1)} %get-tuple-element.156), channel_id=1, source_target_pairs={{1,0},{3,2},{5,4},{7,6},{9,8},{11,10},{13,12},{15,14},{17,16},{19,... | collective-permute-start | bytes 205928 | tf_op jit(solution)/shard_map/ppermute | solution.py:20
  381.8 9.6 %collective-permute-start.47 = (f32[2,1,66,130]{3,2,1,0:T(8,128)S(1)}, f32[2,1,66,130]{3,2,1,0:T(8,128)S(1)}, u32[]{:S(2)}, u32[]{:S(2)}) collective-permute-start(f32[2,1,66,130]{3,2,1,0:T(8,128)S(1)} %get-tuple-element.157), channel_id=1, source_target_pairs={{0,1},{2,3},{4,5},{6,7},{8,9},{10,11},{12,13},{14,15},{16,17},{18,... | collective-permute-start | bytes 205928 | tf_op jit(solution)/shard_map/ppermute | solution.py:19
  405.0 8.9 %collective-permute-start.50 = (f32[2,2,66,1]{3,2,1,0:T(8,128)S(1)}, f32[2,2,66,1]{3,2,1,0:T(8,128)S(1)}, u32[]{:S(2)}, u32[]{:S(2)}) collective-permute-start(f32[2,2,66,1]{3,2,1,0:T(8,128)S(1)} %get-tuple-element.179), channel_id=1, source_target_pairs={{0,2},{2,4},{4,6},{6,8},{8,10},{10,12},{12,14},{1,3},{3,5},{5,7},{... | collective-permute-start | bytes 3176 | tf_op jit(solution)/shard_map/ppermute | solution.py:19
  435.4 14.1 %collective-permute-start.56 = (f32[2,2,66,1]{3,2,1,0:T(8,128)S(1)}, f32[2,2,66,1]{3,2,1,0:T(8,128)S(1)}, u32[]{:S(2)}, u32[]{:S(2)}) collective-permute-start(f32[2,2,66,1]{3,2,1,0:T(8,128)S(1)} %get-tuple-element.177), channel_id=1, source_target_pairs={{0,2},{2,4},{4,6},{6,8},{8,10},{10,12},{12,14},{1,3},{3,5},{5,7},{... | collective-permute-start | bytes 3176 | tf_op jit(solution)/shard_map/ppermute | solution.py:19
  440.6 9.0 %collective-permute-start.57 = (f32[2,2,66,1]{3,2,1,0:T(8,128)S(1)}, f32[2,2,66,1]{3,2,1,0:T(8,128)S(1)}, u32[]{:S(2)}, u32[]{:S(2)}) collective-permute-start(f32[2,2,66,1]{3,2,1,0:T(8,128)S(1)} %get-tuple-element.176), channel_id=1, source_target_pairs={{2,0},{4,2},{6,4},{8,6},{10,8},{12,10},{14,12},{3,1},{5,3},{7,5},{... | collective-permute-start | bytes 3176 | tf_op jit(solution)/shard_map/ppermute | solution.py:20
  442.5 12.7 %collective-permute-start.66 = (f32[2,2,1,128]{3,2,1,0:T(1,128)S(1)}, f32[2,2,1,128]{3,2,1,0:T(1,128)S(1)}, u32[]{:S(2)}, u32[]{:S(2)}) collective-permute-start(f32[2,2,1,128]{3,2,1,0:T(1,128)S(1)} %get-tuple-element.202), channel_id=1, source_target_pairs={{0,16},{16,32},{32,48},{48,64},{64,80},{80,96},{96,112},{112,128},... | collective-permute-start | bytes 6152 | tf_op jit(solution)/shard_map/ppermute | solution.py:19
  457.6 13.7 %collective-permute-start.60 = (f32[2,2,1,128]{3,2,1,0:T(1,128)S(1)}, f32[2,2,1,128]{3,2,1,0:T(1,128)S(1)}, u32[]{:S(2)}, u32[]{:S(2)}) collective-permute-start(f32[2,2,1,128]{3,2,1,0:T(1,128)S(1)} %get-tuple-element.204), channel_id=1, source_target_pairs={{0,16},{16,32},{32,48},{48,64},{64,80},{80,96},{96,112},{112,128},... | collective-permute-start | bytes 6152 | tf_op jit(solution)/shard_map/ppermute | solution.py:19
  463.9 13.2 %collective-permute-start.68 = (f32[2,2,66,1]{3,2,1,0:T(8,128)S(1)}, f32[2,2,66,1]{3,2,1,0:T(8,128)S(1)}, u32[]{:S(2)}, u32[]{:S(2)}) collective-permute-start(f32[2,2,66,1]{3,2,1,0:T(8,128)S(1)} %get-tuple-element.173), channel_id=1, source_target_pairs={{0,2},{2,4},{4,6},{6,8},{8,10},{10,12},{12,14},{1,3},{3,5},{5,7},{... | collective-permute-start | bytes 3176 | tf_op jit(solution)/shard_map/ppermute | solution.py:19
  481.8 10.8 %collective-permute-start.64 = (f32[2,1,66,130]{3,2,1,0:T(8,128)S(1)}, f32[2,1,66,130]{3,2,1,0:T(8,128)S(1)}, u32[]{:S(2)}, u32[]{:S(2)}) collective-permute-start(f32[2,1,66,130]{3,2,1,0:T(8,128)S(1)} %get-tuple-element.144), channel_id=1, source_target_pairs={{1,0},{3,2},{5,4},{7,6},{9,8},{11,10},{13,12},{15,14},{17,16},{19,... | collective-permute-start | bytes 205928 | tf_op jit(solution)/shard_map/ppermute | solution.py:20
  483.1 9.5 %collective-permute-start.65 = (f32[2,1,66,130]{3,2,1,0:T(8,128)S(1)}, f32[2,1,66,130]{3,2,1,0:T(8,128)S(1)}, u32[]{:S(2)}, u32[]{:S(2)}) collective-permute-start(f32[2,1,66,130]{3,2,1,0:T(8,128)S(1)} %get-tuple-element.145), channel_id=1, source_target_pairs={{0,1},{2,3},{4,5},{6,7},{8,9},{10,11},{12,13},{14,15},{16,17},{18,... | collective-permute-start | bytes 205928 | tf_op jit(solution)/shard_map/ppermute | solution.py:19
  487.3 125.3 %collective-permute-start.70 = (f32[2,1,66,130]{3,2,1,0:T(8,128)S(1)}, f32[2,1,66,130]{3,2,1,0:T(8,128)S(1)}, u32[]{:S(2)}, u32[]{:S(2)}) collective-permute-start(f32[2,1,66,130]{3,2,1,0:T(8,128)S(1)} %get-tuple-element.142), channel_id=1, source_target_pairs={{1,0},{3,2},{5,4},{7,6},{9,8},{11,10},{13,12},{15,14},{17,16},{19,... | collective-permute-start | bytes 205928 | tf_op jit(solution)/shard_map/ppermute | solution.py:20
  488.6 124.0 %collective-permute-start.71 = (f32[2,1,66,130]{3,2,1,0:T(8,128)S(1)}, f32[2,1,66,130]{3,2,1,0:T(8,128)S(1)}, u32[]{:S(2)}, u32[]{:S(2)}) collective-permute-start(f32[2,1,66,130]{3,2,1,0:T(8,128)S(1)} %get-tuple-element.143), channel_id=1, source_target_pairs={{0,1},{2,3},{4,5},{6,7},{8,9},{10,11},{12,13},{14,15},{16,17},{18,... | collective-permute-start | bytes 205928 | tf_op jit(solution)/shard_map/ppermute | solution.py:19
  (70 other events, 711.7 us)
